TPU v7x, 256 devices: a whole 4x4x8 slice. The times are simulated.
256 devices in a mesh: param: 64 (over x, z, y_hi), sensor: 4 (over y_lo, core).
Axes of the slice: x: 4, y: 4 (y_hi: 2, y_lo: 2; y = y_hi * 2 + y_lo), z: 8, core: 2. Of those that a mesh axis runs over, the one named last changes fastest.
Arguments:
- readings: bfloat16 [64, 600, 128], P('param', 'sensor'), may hold values from -6 to 6
- spectra: bfloat16 [2, 65, 600, 8192], P(None, None, 'sensor', 'param'), may hold values from -0.0625 to 0.0625
- stiffness: float32 [8192], P('param'), may hold values from 0.04 to 0.24
Outputs:
- hessian_panel: float32 [64, 600, 128], P('param', 'sensor')
All inputs are finite; a program needn't handle non-finite values.
Results may differ from a plain program's by a relative error of at most 0.0025.
Values may be sent and summed in bfloat16 or wider, within the bound.
No kernel may reach another device: no remote copies, remote signals or barrier semaphores. Data moves between devices by JAX's collectives and lax.ppermute only.
A program may use at most 128 MiB of HBM per device.

v0:
```python
import math
import jax
import jax.numpy as jnp
from jax import lax
from jax.sharding import PartitionSpec as P

STEPS = 64
GY = 64
NCOL = 128


def with_halo(block, sides, width):
    for axis, dim in sides:
        count = lax.axis_size(axis)
        forward = [(i, i + 1) for i in range(count - 1)]
        backward = [(target, source) for source, target in forward]
        low = lax.ppermute(
            lax.slice_in_dim(block, block.shape[dim] - width, None, axis=dim), axis, forward
        )
        high = lax.ppermute(lax.slice_in_dim(block, 0, width, axis=dim), axis, backward)
        block = jnp.concatenate([low, block, high], axis=dim)
    return block


def angles(bins, times):
    prod = bins[:, None] * times[None, :] % (2 * STEPS)
    return prod.astype(jnp.float32) * (2.0 * math.pi / (2 * STEPS))


def accumulate(loop_carry, piece):
    count = piece.shape[0]
    bins = jnp.arange(STEPS + 1, dtype=jnp.int32)
    times = jnp.arange(count, dtype=jnp.int32)
    phase_angle = angles(bins, times)
    scale_factor = 1.0 / math.sqrt(STEPS)
    value_entries = piece.astype(jnp.float32)
    hessian_product = lax.Precision.HIGHEST
    real_part = jnp.einsum(
        "uo,ojm->ujm", jnp.cos(phase_angle) * scale_factor, value_entries, precision=hessian_product
    )
    imaginary_part = loop_carry[1] - jnp.einsum(
        "uo,ojm->ujm", jnp.sin(phase_angle) * scale_factor, value_entries, precision=hessian_product
    )
    return (real_part, imaginary_part)


def inverse_rows(real_part, imaginary_part, count):
    bins = jnp.arange(STEPS + 1, dtype=jnp.int32)
    times = jnp.arange(count, dtype=jnp.int32)
    phase_angle = angles(bins, times)
    weight = jnp.where((bins == 0) | (bins == STEPS), 1.0, 2.0).astype(jnp.float32)[:, None]
    scale_factor = 1.0 / math.sqrt(STEPS)
    hessian_product = lax.Precision.HIGHEST
    cosine_inverse = (jnp.cos(phase_angle) * weight * scale_factor).T
    sine_inverse = (jnp.sin(phase_angle) * weight * scale_factor).T
    return jnp.einsum(
        "ni,ilj->nlj", cosine_inverse, real_part, precision=hessian_product
    ) - jnp.einsum("ni,ilj->nlj", sine_inverse, imaginary_part, precision=hessian_product)


def sweep_once(grid, coeff):
    padded = with_halo(grid.astype(jnp.bfloat16), (("param", 1),), 1).astype(grid.dtype)
    sides = jnp.pad(grid, ((0, 0), (0, 0), (1, 1), (0, 0)))
    beside_all = padded[:, :-2] + padded[:, 2:] + sides[:, :, :-2] + sides[:, :, 2:]
    return grid + coeff * (beside_all - 4.0 * grid)


def shards(readings, spectra, stiffness):
    sens_rows = readings.shape[1]
    points = spectra.shape[3]
    rows_here = points // GY
    empty_data = jnp.zeros((STEPS + 1, sens_rows, NCOL), jnp.float32)
    data_re, data_im = accumulate(
        (empty_data, empty_data), lax.all_gather(readings, "param", axis=0, tiled=True)
    )
    data_re = data_re.astype(jnp.bfloat16)
    data_im = data_im.astype(jnp.bfloat16)
    spectrum_real = spectra[0]
    spectrum_imaginary = spectra[1]
    f32 = jnp.float32
    adj_re = jnp.einsum(
        "ksm,ksc->kmc", spectrum_real, data_re, preferred_element_type=f32
    ) + jnp.einsum("ksm,ksc->kmc", spectrum_imaginary, data_im, preferred_element_type=f32)
    adj_im = jnp.einsum(
        "ksm,ksc->kmc", spectrum_real, data_im, preferred_element_type=f32
    ) - jnp.einsum("ksm,ksc->kmc", spectrum_imaginary, data_re, preferred_element_type=f32)
    field = inverse_rows(adj_re, adj_im, STEPS)
    grid = field.reshape(STEPS, rows_here, GY, NCOL)
    coeff = stiffness.reshape(rows_here, GY)[None, :, :, None]
    empty_model = jnp.zeros((STEPS + 1, points, NCOL), jnp.float32)
    grid = lax.psum(grid, "sensor")
    for sweep in range(2):
        grid = sweep_once(grid, coeff)
    model_re, model_im = accumulate((empty_model, empty_model), grid.reshape(STEPS, points, NCOL))
    model_re = model_re.astype(jnp.bfloat16)
    model_im = model_im.astype(jnp.bfloat16)
    out_re = jnp.einsum(
        "ksm,kmc->ksc", spectrum_real, model_re, preferred_element_type=f32
    ) - jnp.einsum("ksm,kmc->ksc", spectrum_imaginary, model_im, preferred_element_type=f32)
    out_im = jnp.einsum(
        "ksm,kmc->ksc", spectrum_real, model_im, preferred_element_type=f32
    ) + jnp.einsum("ksm,kmc->ksc", spectrum_imaginary, model_re, preferred_element_type=f32)
    return lax.psum_scatter(
        inverse_rows(out_re, out_im, readings.shape[0] * lax.axis_size("param")),
        "param",
        scatter_dimension=0,
        tiled=True,
    )


def solution(mesh):
    return jax.shard_map(
        shards,
        mesh=mesh,
        in_specs=(P("param", "sensor", None), P(None, None, "sensor", "param"), P("param")),
        out_specs=P("param", "sensor", None),
        check_vma=False,
    )
```

profile of v0, /device:TPU:8, one launch (start us, length us, event | category | flops | bytes accessed | tf_op | source)
XLA Modules:
  0.0 807.7 jit_solution(7636657847180767540)
XLA Ops:
  6.5 0.0 all-gather.2.cloned.1.call-start
  6.5 0.7 all-gather.2.cloned.1.call-update
  7.3 0.0 all-reduce.5.cloned.1.call-start
  7.3 10.1 %fusion.120 = (bf16[1,65,150,128]{3,0,2,1:T(2,128)(2,1)S(1)}, bf16[1,65,150,128]{3,0,2,1:T(2,128)(2,1)S(1)}) fusion(bf16[2,65,150,128]{3,0,2,1:T(2,128)(2,1)} %param.4), kind=kLoop, calls=%fused_computation.126 | loop fusion | bytes 9984000 | tf_op jit(solution)/shard_map/slice | solution.py:79
  17.5 2.7 copy_bitcast_fusion
  20.2 112.0 %all-gather.2.cloned.1.call-done = bf16[64,150,128]{2,1,0:T(8,128)(2,1)} async-done(((bf16[1,150,128]{2,1,0:T(8,128)(2,1)}), bf16[64,150,128]{2,1,0:T(8,128)(2,1)}) %all-gather.2.cloned.1.call-update) | async-done | bytes 2457616 | tf_op jit(solution)/shard_map/all_gather | solution.py:74
  132.2 0.0 copy-start
  132.2 4.4 fusion.19
  136.6 0.0 copy-start.2
  136.6 0.0 copy-done
  136.7 0.0 copy-start.6
  136.7 1.5 fusion.25
  138.1 1.3 copy-done.2
  139.4 0.8 copy-done.6
  140.2 2.5 fusion.21
  142.8 3.4 fusion.23
  146.2 3.4 subtract_bitcast_fusion.1
  149.6 6.0 copy.33
  155.7 7.6 add_bitcast_fusion.1
  163.2 5.6 copy.32
  168.8 0.0 copy-start.3
  168.8 6.0 fusion.43
  174.8 0.0 copy-done.3
  174.8 5.6 convolution_subtract_fusion
  180.4 0.0 all-reduce.5.cloned.1.call-update
  180.5 0.0 copy-start.7
  180.5 0.0 reduce-scatter.5.cloned.1.call-start
  180.5 92.4 %all-reduce.5.cloned.1.call-done = f32[64,2,64,128]{3,0,2,1:T(8,128)} async-done(((f32[64,2,64,128]{3,0,2,1:T(8,128)}), f32[64,2,64,128]{3,0,2,1:T(8,128)}) %all-reduce.5.cloned.1.call-update) | async-done | bytes 4194320 | tf_op jit(solution)/shard_map/psum | solution.py:91
  272.9 2.7 convert_element_type.51
  275.6 0.0 copy-start.4
  275.6 1.3 copy-done.4
  277.0 1.6 fusion.122
  278.5 6.0 collective-permute-start
  284.5 1.3 collective-permute-start.1
  285.8 0.0 copy-done.7
  285.8 0.1 mul.185
  285.9 0.0 copy-start.5
  285.9 43.3 %collective-permute-done = bf16[64,1,64,128]{3,0,2,1:T(8,128)(2,1)} collective-permute-done((bf16[64,1,64,128]{3,0,2,1:T(8,128)(2,1)}, bf16[64,1,64,128]{3,0,2,1:T(8,128)(2,1)}, u32[]{:S(2)}, u32[]{:S(2)}) %collective-permute-start) | collective-permute-done | bytes 1048608 | tf_op jit(solution)/shard_map/ppermute | solution.py:17
  329.2 0.0 collective-permute-done.1
  329.2 2.5 maximum_convert_fusion
  331.7 0.0 copy-done.5
  331.7 1.2 fusion.118
  332.9 0.2 fusion.121
  333.1 6.0 collective-permute-start.2
  339.1 1.3 collective-permute-start.3
  340.4 43.2 %collective-permute-done.2 = bf16[64,1,64,128]{3,0,2,1:T(8,128)(2,1)S(1)} collective-permute-done((bf16[64,1,64,128]{3,0,2,1:T(8,128)(2,1)S(1)}, bf16[64,1,64,128]{3,0,2,1:T(8,128)(2,1)S(1)}, u32[]{:S(2)}, u32[]{:S(2)}) %collective-permute-start.2) | collective-permute-done | bytes 1048608 | tf_op jit(solution)/shard_map/ppermute | solution.py:17
  383.6 0.0 collective-permute-done.3
  383.6 0.7 maximum_convert_fusion.1
  384.3 1.1 fusion.10
  385.3 4.6 fusion.39
  390.0 0.0 copy-start.1
  390.0 4.4 fusion.36
  394.4 0.0 copy-done.1
  394.4 1.5 fusion.28
  395.9 1.5 fusion.24
  397.4 1.5 add_bitcast_fusion
  398.9 5.8 fusion
  404.7 1.6 subtract_bitcast_fusion
  406.3 5.6 fusion.16
  411.9 5.1 copy.38
  417.0 0.0 reduce-scatter.5.cloned.1.call-update
  417.0 382.3 %reduce-scatter.5.cloned.1.call-done = f32[1,150,128]{2,1,0:T(8,128)} async-done(((f32[64,150,128]{2,1,0:T(8,128)}), f32[1,150,128]{2,1,0:T(8,128)}) %reduce-scatter.5.cloned.1.call-update) | async-done | bytes 76816
  799.3 1.6 copy.39
  (1 shorter events, 0.0 us)
Async XLA Ops:
  6.5 125.7 %all-gather.2.cloned.1.call-start = ((), (), s32[]{:S(2)}) async-start(), calls=%async_computation.1 | async-start | bytes 2529280 | tf_op jit(solution)/shard_map/all_gather | solution.py:74
  7.3 265.7 %all-reduce.5.cloned.1.call-start = ((), (), s32[]{:S(2)}) async-start(), calls=%async_computation.2 | async-start | bytes 8388608 | tf_op jit(solution)/shard_map/psum | solution.py:91
  132.2 4.4 copy-start
  136.6 2.8 copy-start.2
  136.7 3.6 copy-start.6
  168.8 6.0 copy-start.3
  180.5 105.3 %copy-start.7 = (f32[128]{0:T(128)S(1)}, f32[128]{0:T(128)}, u32[]{:S(2)}) copy-start(f32[128]{0:T(128)} %param.5) | copy-start | bytes 1540
  180.5 618.9 %reduce-scatter.5.cloned.1.call-start = ((), (), s32[]{:S(2)}) async-start(), calls=%async_computation.3 | async-start | bytes 5058560
  275.6 1.4 copy-start.4
  278.5 50.7 %collective-permute-start = (bf16[64,1,64,128]{3,0,2,1:T(8,128)(2,1)}, bf16[64,1,64,128]{3,0,2,1:T(8,128)(2,1)}, u32[]{:S(2)}, u32[]{:S(2)}) collective-permute-start(bf16[64,1,64,128]{3,0,2,1:T(8,128)(2,1)} %get-tuple-element.11), channel_id=1, source_target_pairs={{0,4},{4,8},{8,12},{12,16},{16,20},{20,24},{24,28},{28,32},{32,36}... | collective-permute-start | bytes 3145736 | tf_op jit(solution)/shard_map/ppermute | solution.py:17
  284.5 44.7 %collective-permute-start.1 = (bf16[64,1,64,128]{3,0,2,1:T(8,128)(2,1)}, bf16[64,1,64,128]{3,0,2,1:T(8,128)(2,1)}, u32[]{:S(2)}, u32[]{:S(2)}) collective-permute-start(bf16[64,1,64,128]{3,0,2,1:T(8,128)(2,1)} %get-tuple-element.12), channel_id=1, source_target_pairs={{4,0},{8,4},{12,8},{16,12},{20,16},{24,20},{28,24},{32,28},{36,32}... | collective-permute-start | bytes 3145736 | tf_op jit(solution)/shard_map/ppermute | solution.py:20
  285.9 45.8 %copy-start.5 = (f32[64,2,64,128]{3,0,2,1:T(8,128)S(1)}, f32[64,2,64,128]{3,0,2,1:T(8,128)}, u32[]{:S(2)}) copy-start(f32[64,2,64,128]{3,0,2,1:T(8,128)} %all-reduce.5.cloned.1.call-done) | copy-start | bytes 12582916
  333.1 50.5 %collective-permute-start.2 = (bf16[64,1,64,128]{3,0,2,1:T(8,128)(2,1)S(1)}, bf16[64,1,64,128]{3,0,2,1:T(8,128)(2,1)S(1)}, u32[]{:S(2)}, u32[]{:S(2)}) collective-permute-start(bf16[64,1,64,128]{3,0,2,1:T(8,128)(2,1)S(1)} %get-tuple-element.9), channel_id=1, source_target_pairs={{0,4},{4,8},{8,12},{12,16},{16,20},{20,24},{24,28},{28,32},{32,36}... | collective-permute-start | bytes 3145736 | tf_op jit(solution)/shard_map/ppermute | solution.py:17
  339.1 44.5 %collective-permute-start.3 = (bf16[64,1,64,128]{3,0,2,1:T(8,128)(2,1)S(1)}, bf16[64,1,64,128]{3,0,2,1:T(8,128)(2,1)S(1)}, u32[]{:S(2)}, u32[]{:S(2)}) collective-permute-start(bf16[64,1,64,128]{3,0,2,1:T(8,128)(2,1)S(1)} %get-tuple-element.10), channel_id=1, source_target_pairs={{4,0},{8,4},{12,8},{16,12},{20,16},{24,20},{28,24},{32,28},{36,32}... | collective-permute-start | bytes 3145736 | tf_op jit(solution)/shard_map/ppermute | solution.py:20
  390.0 4.4 copy-start.1
Sparse Core Ops, SparseCore 0:
  10.8 121.3 all-gather.1
  180.6 92.2 all-reduce.4
  417.1 382.1 reduce-scatter.4
where the time goes:
time: 816 us; the launch traced here: 808 us
  waiting for transfers between devices  674 us (83%)
  matrix products  60.9 us (7%)
  local copies, waits for them, and re-layouts  36.4 us (4%)
  starting transfers between devices  14.6 us (2%)
  between operations  13.6 us (2%)
    unnamed x4, waiting for transfers between devices  383 us
    all_gather x1, waiting for transfers between devices, shards(): lax.all_gather(readings, 'param', axis=0, tiled=True)  112 us
    psum x1, waiting for transfers between devices, shards(): grid = lax.psum(grid, 'sensor')  92.4 us
    ppermute x2, waiting for transfers between devices, with_halo(): lax.ppermute(lax.slice_in_dim(block, block.shape[dim] - width, None, axis...  86.6 us
  transfers between devices with their start and end apart: 7, of which 5 were waited for; matrix products, arithmetic and copies ran while one was open for 2% of the time, Pallas kernels for 0%

commit v1 on v0

--- a/solution.py
+++ b/solution.py
@@ -71,7 +71,10 @@
     rows_here = points // GY
     empty_data = jnp.zeros((STEPS + 1, sens_rows, NCOL), jnp.float32)
     data_re, data_im = accumulate(
-        (empty_data, empty_data), lax.all_gather(readings, "param", axis=0, tiled=True)
+        (empty_data, empty_data),
+        jnp.concatenate(
+            lax.all_to_all(jnp.stack([readings] * lax.axis_size("param")), "param", 0, 0), axis=0
+        ),
     )
     data_re = data_re.astype(jnp.bfloat16)
     data_im = data_im.astype(jnp.bfloat16)

time: 816 us -> 769 us (0.942)
  waiting for transfers between devices: 674 us -> 607 us
  starting transfers between devices: 14.6 us -> 28.5 us
    all_gather x1 -> x0, waiting for transfers between devices: 112 us -> none  [shards(): lax.all_gather(readings, 'param', axis=0, tiled=True)]
    all_to_all x0 -> x1, waiting for transfers between devices: none -> 48.5 us  [shards(): lax.all_to_all(jnp.stack([readings] * lax.axis_size('param')), 'param', 0...]
    all_to_all x0 -> x1, starting transfers between devices: none -> 13.9 us  [shards(): lax.all_to_all(jnp.stack([readings] * lax.axis_size('param')), 'param', 0...]
    unnamed x4 -> x3, waiting for transfers between devices: 383 us -> 382 us
where the time goes in v1:
time: 769 us; the launch traced here: 760 us
  waiting for transfers between devices  607 us (79%)
  matrix products  63.8 us (8%)
  local copies, waits for them, and re-layouts  38.7 us (5%)
  starting transfers between devices  28.5 us (4%)
  between operations  14.1 us (2%)
  other arithmetic  8.24 us (1%)
    unnamed x3, waiting for transfers between devices  382 us
    psum x1, waiting for transfers between devices, shards(): grid = lax.psum(grid, 'sensor')  89.8 us
    ppermute x2, waiting for transfers between devices, with_halo(): lax.ppermute(lax.slice_in_dim(block, block.shape[dim] - width, None, axis...  86.6 us
    all_to_all x1, waiting for transfers between devices, shards(): lax.all_to_all(jnp.stack([readings] * lax.axis_size('param')), 'param', 0...  48.5 us
  transfers between devices with their start and end apart: 7, of which 5 were waited for; matrix products, arithmetic and copies ran while one was open for 2% of the time, Pallas kernels for 0%

profile of v1, /device:TPU:8, one launch (start us, length us, event | category | flops | bytes accessed | tf_op | source)
XLA Modules:
  0.0 759.8 jit_solution(13633857866862219203)
XLA Ops:
  6.5 2.6 stack.2
  9.1 13.9 %all-to-all-start = ((bf16[64,1,150,128]{3,2,1,0:T(8,128)(2,1)}), bf16[64,1,150,128]{3,2,1,0:T(8,128)(2,1)}, u32[]{:S(2)}, u32[]{:S(2)}) async-start(bf16[64,1,150,128]{3,2,1,0:T(8,128)(2,1)} %stack.2), calls=%async_computation | async-start | bytes 4980736 | tf_op jit(solution)/shard_map/all_to_all | solution.py:76
  23.0 0.0 all-reduce.5.cloned.1.call-start
  23.1 10.1 %fusion.122 = (bf16[1,65,150,128]{3,0,2,1:T(2,128)(2,1)S(1)}, bf16[1,65,150,128]{3,0,2,1:T(2,128)(2,1)S(1)}) fusion(bf16[2,65,150,128]{3,0,2,1:T(2,128)(2,1)} %param.4), kind=kLoop, calls=%fused_computation.128 | loop fusion | bytes 9984000 | tf_op jit(solution)/shard_map/slice | solution.py:82
  33.2 2.8 copy_bitcast_fusion
  36.0 48.5 %all-to-all-done = bf16[64,1,150,128]{3,2,1,0:T(8,128)(2,1)} async-done(((bf16[64,1,150,128]{3,2,1,0:T(8,128)(2,1)}), bf16[64,1,150,128]{3,2,1,0:T(8,128)(2,1)}, u32[]{:S(2)}, u32[]{:S(2)}) %all-to-all-start) | async-done | bytes 2457632 | tf_op jit(solution)/shard_map/all_to_all | solution.py:76
  84.4 0.0 copy-start
  84.4 4.4 fusion.16
  88.8 0.0 copy-start.2
  88.8 0.0 copy-done
  88.8 1.5 fusion.27
  90.3 0.9 copy-done.2
  91.2 4.2 fusion.18
  95.5 3.4 fusion.25
  98.9 3.4 subtract_bitcast_fusion.1
  102.3 6.0 copy.29
  108.4 7.6 add_bitcast_fusion.1
  116.0 5.6 copy.28
  121.6 0.0 copy-start.4
  121.6 6.0 fusion.45
  127.5 0.0 copy-done.4
  127.5 5.6 convolution_subtract_fusion
  133.2 0.0 all-reduce.5.cloned.1.call-update
  133.2 0.0 copy-start.7
  133.2 0.0 reduce-scatter.5.cloned.1.call-start
  133.2 89.8 %all-reduce.5.cloned.1.call-done = f32[64,2,64,128]{3,0,2,1:T(8,128)} async-done(((f32[64,2,64,128]{3,0,2,1:T(8,128)}), f32[64,2,64,128]{3,0,2,1:T(8,128)}) %all-reduce.5.cloned.1.call-update) | async-done | bytes 4194320 | tf_op jit(solution)/shard_map/psum | solution.py:94
  223.0 2.7 convert_element_type.51
  225.7 0.0 copy-start.5
  225.7 1.4 copy-done.5
  227.1 1.6 fusion.124
  228.6 6.0 collective-permute-start
  234.6 1.3 collective-permute-start.1
  235.9 0.0 copy-done.7
  235.9 0.1 mul.185
  236.0 0.0 copy-start.6
  236.0 43.3 %collective-permute-done = bf16[64,1,64,128]{3,0,2,1:T(8,128)(2,1)} collective-permute-done((bf16[64,1,64,128]{3,0,2,1:T(8,128)(2,1)}, bf16[64,1,64,128]{3,0,2,1:T(8,128)(2,1)}, u32[]{:S(2)}, u32[]{:S(2)}) %collective-permute-start) | collective-permute-done | bytes 1048608 | tf_op jit(solution)/shard_map/ppermute | solution.py:17
  279.3 0.0 collective-permute-done.1
  279.3 2.5 maximum_convert_fusion
  281.8 0.0 copy-done.6
  281.8 1.2 fusion.120
  283.0 0.2 fusion.123
  283.2 6.0 collective-permute-start.2
  289.2 1.3 collective-permute-start.3
  290.5 43.2 %collective-permute-done.2 = bf16[64,1,64,128]{3,0,2,1:T(8,128)(2,1)S(1)} collective-permute-done((bf16[64,1,64,128]{3,0,2,1:T(8,128)(2,1)S(1)}, bf16[64,1,64,128]{3,0,2,1:T(8,128)(2,1)S(1)}, u32[]{:S(2)}, u32[]{:S(2)}) %collective-permute-start.2) | collective-permute-done | bytes 1048608 | tf_op jit(solution)/shard_map/ppermute | solution.py:17
  333.7 0.0 collective-permute-done.3
  333.7 0.8 maximum_convert_fusion.1
  334.6 1.1 fusion.10
  335.6 4.4 fusion.41
  340.1 0.0 copy-start.1
  340.1 4.4 fusion.38
  344.5 0.0 copy-done.1
  344.5 1.5 fusion.30
  346.0 1.5 fusion.26
  347.4 1.5 add_bitcast_fusion
  349.0 7.3 fusion
  356.3 0.0 copy-start.3
  356.3 1.6 subtract_bitcast_fusion
  357.8 0.8 copy-done.3
  358.7 5.6 fusion.20
  364.2 5.1 copy.34
  369.3 0.0 reduce-scatter.5.cloned.1.call-update
  369.3 381.7 %reduce-scatter.5.cloned.1.call-done = f32[1,150,128]{2,1,0:T(8,128)} async-done(((f32[64,150,128]{2,1,0:T(8,128)}), f32[1,150,128]{2,1,0:T(8,128)}) %reduce-scatter.5.cloned.1.call-update) | async-done | bytes 76816
  751.0 1.6 copy.35
  (1 shorter events, 0.0 us)
Async XLA Ops:
  9.1 75.3 %all-to-all-start = ((bf16[64,1,150,128]{3,2,1,0:T(8,128)(2,1)}), bf16[64,1,150,128]{3,2,1,0:T(8,128)(2,1)}, u32[]{:S(2)}, u32[]{:S(2)}) async-start(bf16[64,1,150,128]{3,2,1,0:T(8,128)(2,1)} %stack.2), calls=%async_computation | async-start | bytes 4980736 | tf_op jit(solution)/shard_map/all_to_all | solution.py:76
  23.0 200.0 %all-reduce.5.cloned.1.call-start = ((), (), s32[]{:S(2)}) async-start(), calls=%async_computation.2 | async-start | bytes 8388608 | tf_op jit(solution)/shard_map/psum | solution.py:94
  84.4 4.4 copy-start
  88.8 2.4 copy-start.2
  121.6 6.0 copy-start.4
  133.2 102.7 %copy-start.7 = (f32[128]{0:T(128)S(1)}, f32[128]{0:T(128)}, u32[]{:S(2)}) copy-start(f32[128]{0:T(128)} %param.5) | copy-start | bytes 1540
  133.2 617.8 %reduce-scatter.5.cloned.1.call-start = ((), (), s32[]{:S(2)}) async-start(), calls=%async_computation.3 | async-start | bytes 5058560
  225.7 1.4 copy-start.5
  228.6 50.7 %collective-permute-start = (bf16[64,1,64,128]{3,0,2,1:T(8,128)(2,1)}, bf16[64,1,64,128]{3,0,2,1:T(8,128)(2,1)}, u32[]{:S(2)}, u32[]{:S(2)}) collective-permute-start(bf16[64,1,64,128]{3,0,2,1:T(8,128)(2,1)} %get-tuple-element.11), channel_id=1, source_target_pairs={{0,4},{4,8},{8,12},{12,16},{16,20},{20,24},{24,28},{28,32},{32,36}... | collective-permute-start | bytes 3145736 | tf_op jit(solution)/shard_map/ppermute | solution.py:17
  234.6 44.7 %collective-permute-start.1 = (bf16[64,1,64,128]{3,0,2,1:T(8,128)(2,1)}, bf16[64,1,64,128]{3,0,2,1:T(8,128)(2,1)}, u32[]{:S(2)}, u32[]{:S(2)}) collective-permute-start(bf16[64,1,64,128]{3,0,2,1:T(8,128)(2,1)} %get-tuple-element.12), channel_id=1, source_target_pairs={{4,0},{8,4},{12,8},{16,12},{20,16},{24,20},{28,24},{32,28},{36,32}... | collective-permute-start | bytes 3145736 | tf_op jit(solution)/shard_map/ppermute | solution.py:20
  236.0 45.8 %copy-start.6 = (f32[64,2,64,128]{3,0,2,1:T(8,128)S(1)}, f32[64,2,64,128]{3,0,2,1:T(8,128)}, u32[]{:S(2)}) copy-start(f32[64,2,64,128]{3,0,2,1:T(8,128)} %all-reduce.5.cloned.1.call-done) | copy-start | bytes 12582916
  283.2 50.5 %collective-permute-start.2 = (bf16[64,1,64,128]{3,0,2,1:T(8,128)(2,1)S(1)}, bf16[64,1,64,128]{3,0,2,1:T(8,128)(2,1)S(1)}, u32[]{:S(2)}, u32[]{:S(2)}) collective-permute-start(bf16[64,1,64,128]{3,0,2,1:T(8,128)(2,1)S(1)} %get-tuple-element.9), channel_id=1, source_target_pairs={{0,4},{4,8},{8,12},{12,16},{16,20},{20,24},{24,28},{28,32},{32,36}... | collective-permute-start | bytes 3145736 | tf_op jit(solution)/shard_map/ppermute | solution.py:17
  289.2 44.5 %collective-permute-start.3 = (bf16[64,1,64,128]{3,0,2,1:T(8,128)(2,1)S(1)}, bf16[64,1,64,128]{3,0,2,1:T(8,128)(2,1)S(1)}, u32[]{:S(2)}, u32[]{:S(2)}) collective-permute-start(bf16[64,1,64,128]{3,0,2,1:T(8,128)(2,1)S(1)} %get-tuple-element.10), channel_id=1, source_target_pairs={{4,0},{8,4},{12,8},{16,12},{20,16},{24,20},{28,24},{32,28},{36,32}... | collective-permute-start | bytes 3145736 | tf_op jit(solution)/shard_map/ppermute | solution.py:20
  340.1 4.4 copy-start.1
  356.3 2.4 copy-start.3
Sparse Core Ops, SparseCore 0:
  133.3 89.6 all-reduce.4
  369.4 381.5 reduce-scatter.4
